TPU v7x, 32 devices: a whole 2x2x4 slice. The times are simulated.
32 devices in a mesh: row: 8 (over z, y), col: 4 (over x, core).
Axes of the slice: x: 2, y: 2, z: 4, core: 2. Of those that a mesh axis runs over, the one named last changes fastest.
Arguments:
- tokens_in: bfloat16 [10240, 1024], P('row', 'col'), may hold values from -6 to 6
- grad_out: bfloat16 [10240, 1024], P('row', 'col'), may hold values from -6 to 6
- keep_mask: int32 [32, 256], P('row'), may hold values 0 or 1
- adapter_index: int32 [32], P('row'), may hold values from 0 to 7
- ln_gain: float32 [2, 1024], replicated, may hold values from 0.25 to 1.75
- ln_shift: float32 [2, 1024], replicated, may hold values from -1.8 to 1.8
- w_qkv: bfloat16 [3, 1024, 1024], P(None, 'row', 'col'), may hold values from -0.1875 to 0.1875
- bias_qv: bfloat16 [2, 1024], P(None, 'col'), may hold values from -1.796875 to 1.796875
- w_proj: bfloat16 [1024, 1024], P('col', 'row'), may hold values from -1.5 to 1.5
- w_fc1: bfloat16 [1024, 4096], P('row', 'col'), may hold values from -0.1875 to 0.1875
- bias_fc1: bfloat16 [4096], P('col'), may hold values from -1.796875 to 1.796875
- w_fc2: bfloat16 [4096, 1024], P('col', 'row'), may hold values from -0.09375 to 0.09375
- bias_out: bfloat16 [2, 1024], replicated, may hold values from -1.796875 to 1.796875
- qkv_down: bfloat16 [8, 16, 1024], replicated, may hold values from -0.1875 to 0.1875
- qkv_up: bfloat16 [8, 16, 3, 1024], replicated, may hold values from -0.75 to 0.75
- proj_down: bfloat16 [8, 16, 1024], replicated, may hold values from -1.5 to 1.5
- proj_up: bfloat16 [8, 16, 1024], replicated, may hold values from -0.75 to 0.75
- fc1_down: bfloat16 [8, 16, 1024], replicated, may hold values from -0.1875 to 0.1875
- fc1_up: bfloat16 [8, 16, 4096], replicated, may hold values from -0.75 to 0.75
- fc2_down: bfloat16 [8, 16, 4096], replicated, may hold values from -0.09375 to 0.09375
- fc2_up: bfloat16 [8, 16, 1024], replicated, may hold values from -0.75 to 0.75
Outputs:
- layer_out: bfloat16 [10240, 1024], P('row', 'col')
- grad_in: bfloat16 [10240, 1024], P('row', 'col')
- grad_qkv_down: float32 [8, 16, 1024], replicated
- grad_qkv_up: float32 [8, 16, 3, 1024], replicated
- grad_proj_down: float32 [8, 16, 1024], replicated
- grad_proj_up: float32 [8, 16, 1024], replicated
- grad_fc1_down: float32 [8, 16, 1024], replicated
- grad_fc1_up: float32 [8, 16, 4096], replicated
- grad_fc2_down: float32 [8, 16, 4096], replicated
- grad_fc2_up: float32 [8, 16, 1024], replicated
All inputs are finite; a program needn't handle non-finite values. No bound on the sum of `keep_mask` on one device may be relied on, other than what follows from the above.
Results may differ from a plain program's by a relative error of at most 0.013.
Values may be sent and summed in bfloat16 or wider, within the bound.
No kernel may reach another device: no remote copies, remote signals or barrier semaphores. Data moves between devices by JAX's collectives and lax.ppermute only.
A program may use at most 192 MiB of HBM per device.

v0:
```python
import jax
import jax.numpy as jnp
from jax import lax
from jax.sharding import PartitionSpec as P

D = 1024
H = 16
HD = 64
FF = 4096
BUF = 64
R = 16
NA = 8
SEQ = 320
highest = lax.Precision.HIGHEST


def norm_parts(values):
    row_mean = jnp.mean(values, axis=-1, keepdims=True)
    centered = values - row_mean
    variance = jnp.mean(centered * centered, axis=-1, keepdims=True)
    inverse = lax.rsqrt(variance + 1e-06)
    return (centered * inverse, inverse)


def norm_back(grad_normed, gain_row, unit_rows, inverse):
    scaled = grad_normed * gain_row
    first_mean = jnp.mean(scaled, axis=-1, keepdims=True)
    second_mean = jnp.mean(scaled * unit_rows, axis=-1, keepdims=True)
    return inverse * (scaled - first_mean - unit_rows * second_mean)


def gelu_slope(pre_gelu):
    cumulative = 0.5 * (1.0 + lax.erf(pre_gelu * 0.7071067811865476))
    return cumulative + pre_gelu * jnp.exp(-0.5 * pre_gelu * pre_gelu) * 0.3989422804014327


def narrow_dot(formula, left_side, right_side):
    return jnp.einsum(formula, left_side, right_side, preferred_element_type=jnp.float32)


def exact_dot(formula, left_side, right_side):
    return jnp.einsum(
        formula, left_side, right_side, precision=highest, preferred_element_type=jnp.float32
    )


def attention_pair(query_heads, key_heads, value_heads, key_open):

    def scores_of():
        raw_scores = narrow_dot("gqhd,gkhd->ghqk", query_heads, key_heads) * 0.125
        return jnp.where(key_open[:, None, None, :], raw_scores, -1e30)

    scores = scores_of()
    top_score = jnp.max(scores, axis=-1, keepdims=True)
    exponent = jnp.exp(scores - top_score)
    row_total = jnp.sum(exponent, axis=-1, keepdims=True)
    log_total = top_score + jnp.log(row_total)
    soft_low = (exponent / row_total).astype(jnp.bfloat16)
    attended = narrow_dot("ghqk,gkhd->gqhd", soft_low, value_heads)

    def backward(grad_heads):
        soft_again = jnp.exp(scores_of() - log_total)
        grad_values = narrow_dot("ghqk,gqhd->gkhd", soft_again.astype(jnp.bfloat16), grad_heads)
        grad_soft = narrow_dot("gqhd,gkhd->ghqk", grad_heads, value_heads)
        grad_scores = (
            soft_again * (grad_soft - jnp.sum(grad_soft * soft_again, axis=-1, keepdims=True))
        ).astype(jnp.bfloat16)
        grad_queries = narrow_dot("ghqk,gkhd->gqhd", grad_scores, key_heads) * 0.125
        grad_keys = narrow_dot("ghqk,gqhd->gkhd", grad_scores, query_heads) * 0.125
        return (grad_queries, grad_keys, grad_values)

    return (attended, backward)


def images_layer(
    x_rows,
    g_rows,
    keep_rows,
    select,
    key_open,
    ln_gain,
    ln_shift,
    w_qkv,
    bias_qv,
    w_proj,
    w_fc1,
    bias_fc1,
    w_fc2,
    bias_out,
    flats,
):
    (
        qkv_down_flat,
        qkv_up_flat,
        proj_down_flat,
        proj_up_flat,
        fc1_down_flat,
        fc1_up_flat,
        fc2_down_flat,
        fc2_up_flat,
    ) = flats
    images = key_open.shape[0]
    tok_rows = images * SEQ
    bias_pair = bias_qv.astype(jnp.float32)
    bias_pair_out = bias_out.astype(jnp.float32)
    hidden = x_rows.astype(jnp.float32)
    unit_one, inverse_one = norm_parts(hidden)
    normed_one = (unit_one * ln_gain[0] + ln_shift[0]).astype(jnp.bfloat16)
    latent_one = narrow_dot("td,rd->tr", normed_one, qkv_down_flat) * select
    projected = narrow_dot("td,cde->cte", normed_one, w_qkv) + exact_dot(
        "tr,rce->cte", latent_one, qkv_up_flat.astype(jnp.float32)
    )
    queries = (projected[0] + bias_pair[0]).astype(jnp.bfloat16)
    key_side = projected[1].astype(jnp.bfloat16)
    value_side = (projected[2] + bias_pair[1]).astype(jnp.bfloat16)
    head_shape = (images, SEQ, H, HD)
    attended_heads, attention_back = attention_pair(
        queries.reshape(head_shape),
        key_side.reshape(head_shape),
        value_side.reshape(head_shape),
        key_open,
    )
    attended = attended_heads.reshape(tok_rows, D).astype(jnp.bfloat16)
    latent_two = narrow_dot("th,rh->tr", attended, proj_down_flat) * select
    branch = (
        narrow_dot("th,hd->td", attended, w_proj)
        + exact_dot("tr,rd->td", latent_two, proj_up_flat.astype(jnp.float32))
        + bias_pair_out[0]
    )
    middle = hidden + branch
    unit_two, inverse_two = norm_parts(middle)
    normed_two = (unit_two * ln_gain[1] + ln_shift[1]).astype(jnp.bfloat16)
    latent_three = narrow_dot("td,rd->tr", normed_two, fc1_down_flat) * select
    pre_gelu = (
        narrow_dot("td,df->tf", normed_two, w_fc1)
        + exact_dot("tr,rf->tf", latent_three, fc1_up_flat.astype(jnp.float32))
        + bias_fc1.astype(jnp.float32)
    )
    activated = jax.nn.gelu(pre_gelu, approximate=False).astype(jnp.bfloat16)
    latent_four = narrow_dot("tf,rf->tr", activated, fc2_down_flat) * select
    result = (
        narrow_dot("tf,fd->td", activated, w_fc2)
        + exact_dot("tr,rd->td", latent_four, fc2_up_flat.astype(jnp.float32))
        + bias_pair_out[1]
    )
    out_rows = (keep_rows * (middle + result)).astype(jnp.bfloat16)
    grad_result = g_rows.astype(jnp.float32) * keep_rows
    grad_result_low = grad_result.astype(jnp.bfloat16)
    grad_latent_four = narrow_dot("td,rd->tr", grad_result_low, fc2_up_flat) * select
    grad_act = narrow_dot("td,fd->tf", grad_result_low, w_fc2) + exact_dot(
        "tr,rf->tf", grad_latent_four, fc2_down_flat.astype(jnp.float32)
    )
    grad_pre = (grad_act * gelu_slope(pre_gelu)).astype(jnp.bfloat16)
    grad_latent_three = narrow_dot("tf,rf->tr", grad_pre, fc1_up_flat) * select
    grad_normed_two = narrow_dot("tf,df->td", grad_pre, w_fc1) + exact_dot(
        "tr,rd->td", grad_latent_three, fc1_down_flat.astype(jnp.float32)
    )
    grad_fc2_up = exact_dot("tr,td->rd", latent_four, grad_result)
    grad_fc2_down = exact_dot("tr,tf->rf", grad_latent_four, activated.astype(jnp.float32))
    grad_fc1_up = exact_dot("tr,tf->rf", latent_three, grad_pre.astype(jnp.float32))
    grad_fc1_down = exact_dot("tr,td->rd", grad_latent_three, normed_two.astype(jnp.float32))
    grad_middle = grad_result + norm_back(grad_normed_two, ln_gain[1], unit_two, inverse_two)
    grad_branch = grad_middle.astype(jnp.bfloat16)
    grad_latent_two = narrow_dot("td,rd->tr", grad_branch, proj_up_flat) * select
    grad_attended = (
        narrow_dot("td,hd->th", grad_branch, w_proj)
        + exact_dot("tr,rh->th", grad_latent_two, proj_down_flat.astype(jnp.float32))
    ).astype(jnp.bfloat16)
    grad_proj_up = exact_dot("tr,td->rd", latent_two, grad_branch.astype(jnp.float32))
    grad_proj_down = exact_dot("tr,th->rh", grad_latent_two, attended.astype(jnp.float32))
    grad_queries, grad_keys, grad_values = attention_back(grad_attended.reshape(head_shape))
    grad_qkv = (
        jnp.stack([grad_queries, grad_keys, grad_values])
        .reshape(3, tok_rows, D)
        .astype(jnp.bfloat16)
    )
    grad_latent_one = narrow_dot("cte,rce->tr", grad_qkv, qkv_up_flat) * select
    grad_normed_one = narrow_dot("cte,cde->td", grad_qkv, w_qkv) + exact_dot(
        "tr,rd->td", grad_latent_one, qkv_down_flat.astype(jnp.float32)
    )
    grad_qkv_up = exact_dot("tr,cte->rce", latent_one, grad_qkv.astype(jnp.float32))
    grad_qkv_down = exact_dot("tr,td->rd", grad_latent_one, normed_one.astype(jnp.float32))
    grad_hidden = grad_middle + norm_back(grad_normed_one, ln_gain[0], unit_one, inverse_one)
    grads = (
        grad_qkv_down,
        grad_qkv_up,
        grad_proj_down,
        grad_proj_up,
        grad_fc1_down,
        grad_fc1_up,
        grad_fc2_down,
        grad_fc2_up,
    )
    return (out_rows, grad_hidden.astype(jnp.bfloat16), grads)


def per_device(
    tokens_in,
    grad_out,
    keep_mask,
    adapter_index,
    ln_gain,
    ln_shift,
    w_qkv,
    bias_qv,
    w_proj,
    w_fc1,
    bias_fc1,
    w_fc2,
    bias_out,
    qkv_down,
    qkv_up,
    proj_down,
    proj_up,
    fc1_down,
    fc1_up,
    fc2_down,
    fc2_up,
):
    columns = lax.axis_size("col")
    column = lax.axis_index("col")
    images = adapter_index.shape[0]
    tok_rows = images * SEQ
    rank_total = NA * R
    keep_full = jnp.concatenate([jnp.ones((images, BUF), jnp.int32), keep_mask], axis=1)
    key_open = keep_full > 0
    keep_rows = keep_full.reshape(tok_rows, 1).astype(jnp.float32)
    owner_rows = jnp.broadcast_to(adapter_index[:, None], (images, SEQ)).reshape(tok_rows, 1)
    select = (owner_rows == lax.broadcasted_iota(jnp.int32, (1, rank_total), 1) // R).astype(
        jnp.float32
    )
    flats = (
        qkv_down.reshape(rank_total, D),
        qkv_up.reshape(rank_total, 3, D),
        proj_down.reshape(rank_total, D),
        proj_up.reshape(rank_total, D),
        fc1_down.reshape(rank_total, D),
        fc1_up.reshape(rank_total, FF),
        fc2_down.reshape(rank_total, FF),
        fc2_up.reshape(rank_total, D),
    )
    qkv_cols, proj_rows, fc1_cols, fc2_rows = (
        lax.all_gather(w_qkv, "row", axis=1, tiled=True),
        lax.all_gather(w_proj, "row", axis=1, tiled=True),
        lax.all_gather(w_fc1, "row", axis=0, tiled=True),
        lax.all_gather(w_fc2, "row", axis=1, tiled=True),
    )
    qkv_full, proj_full, fc1_full, fc2_full, bias_qv_full, bias_fc1_full = (
        lax.all_gather(qkv_cols, "col", axis=2, tiled=True),
        lax.all_gather(proj_rows, "col", axis=0, tiled=True),
        lax.all_gather(fc1_cols, "col", axis=1, tiled=True),
        lax.all_gather(fc2_rows, "col", axis=0, tiled=True),
        lax.all_gather(bias_qv, "col", axis=1, tiled=True),
        lax.all_gather(bias_fc1, "col", axis=0, tiled=True),
    )
    x_rows, g_rows = (
        lax.all_to_all(tokens_in, "col", split_axis=0, concat_axis=1, tiled=True),
        lax.all_to_all(grad_out, "col", split_axis=0, concat_axis=1, tiled=True),
    )
    local_images = images // columns
    slice_rows = local_images * SEQ
    row_start = column * slice_rows
    out_rows, grad_rows, grads = images_layer(
        x_rows,
        g_rows,
        lax.dynamic_slice_in_dim(keep_rows, row_start, slice_rows, 0),
        lax.dynamic_slice_in_dim(select, row_start, slice_rows, 0),
        lax.dynamic_slice_in_dim(key_open, column * local_images, local_images, 0),
        ln_gain,
        ln_shift,
        qkv_full,
        bias_qv_full,
        proj_full,
        fc1_full,
        bias_fc1_full,
        fc2_full,
        bias_out,
        flats,
    )
    layer_out, grad_in = (
        lax.all_to_all(out_rows, "col", split_axis=1, concat_axis=0, tiled=True),
        lax.all_to_all(grad_rows, "col", split_axis=1, concat_axis=0, tiled=True),
    )
    summed = lax.psum(
        (grads[0], grads[1], grads[2], grads[3], grads[4], grads[5], grads[6], grads[7]),
        ("row", "col"),
    )
    return (
        layer_out,
        grad_in,
        summed[0].reshape(NA, R, D),
        summed[1].reshape(NA, R, 3, D),
        summed[2].reshape(NA, R, D),
        summed[3].reshape(NA, R, D),
        summed[4].reshape(NA, R, D),
        summed[5].reshape(NA, R, FF),
        summed[6].reshape(NA, R, FF),
        summed[7].reshape(NA, R, D),
    )


def solution(mesh):
    return jax.shard_map(
        per_device,
        mesh=mesh,
        in_specs=(
            P("row", "col"),
            P("row", "col"),
            P("row", None),
            P("row"),
            P(),
            P(),
            P(None, "row", "col"),
            P(None, "col"),
            P("col", "row"),
            P("row", "col"),
            P("col"),
            P("col", "row"),
            P(),
            P(),
            P(),
            P(),
            P(),
            P(),
            P(),
            P(),
            P(),
        ),
        out_specs=(P("row", "col"), P("row", "col"), P(), P(), P(), P(), P(), P(), P(), P()),
        check_vma=False,
    )
```

profile of v0, /device:TPU:0, one launch (start us, length us, event | category | flops | bytes accessed | tf_op | source)
XLA Modules:
  0.0 621.6 jit_solution(14303194922403295950)
XLA Ops:
  9.5 47.7 %all-gather.8.cloned.1.call-done = bf16[3,1024,256]{2,1,0:T(8,128)(2,1)} async-done(((bf16[3,128,256]{2,1,0:T(8,128)(2,1)}), bf16[3,1024,256]{2,1,0:T(8,128)(2,1)}) %all-gather.8.cloned.1.call-update) | async-done | bytes 1572880 | tf_op jit(solution)/shard_map/all_gather | solution.py:243
  57.3 30.8 %all_gather.33 = bf16[256,1024]{1,0:T(8,128)(2,1)} all-gather(bf16[256,128]{1,0:T(8,128)(2,1)} %param.29), channel_id=1, replica_groups=mesh['row'=8,'col'=4] {'row'}, dimensions={1}, use_global_device_ids=true | all-gather | bytes 589824 | tf_op jit(solution)/shard_map/all_gather | solution.py:244
  88.1 21.9 %all-gather.14.cloned.1.call-done = bf16[1024,1024]{1,0:T(8,128)(2,1)} async-done(((bf16[128,1024]{1,0:T(8,128)(2,1)}), bf16[1024,1024]{1,0:T(8,128)(2,1)}) %all-gather.14.cloned.1.call-update) | async-done | bytes 2097168 | tf_op jit(solution)/shard_map/all_gather | solution.py:245
  113.6 11.0 %all_gather.32 = bf16[2,1024]{1,0:T(2,128)(2,1)S(1)} all-gather(bf16[2,256]{1,0:T(2,128)(2,1)S(1)} %copy-done.61), channel_id=1, replica_groups=mesh['row'=8,'col'=4] {'col'}, dimensions={1}, use_global_device_ids=true | all-gather | bytes 5120 | tf_op jit(solution)/shard_map/all_gather | solution.py:253
  124.9 5.2 all_gather.37
  131.6 29.4 %all-gather.18.cloned.1.call-done = bf16[1024,1024]{1,0:T(8,128)(2,1)} async-done(((bf16[1024,128]{1,0:T(8,128)(2,1)}), bf16[1024,1024]{1,0:T(8,128)(2,1)}) %all-gather.18.cloned.1.call-update) | async-done | bytes 2097168 | tf_op jit(solution)/shard_map/all_gather | solution.py:246
  167.2 12.3 %all-to-all-done.2 = bf16[4,320,256]{2,1,0:T(8,128)(2,1)S(1)} async-done(((bf16[4,320,256]{2,1,0:T(8,128)(2,1)}), bf16[4,320,256]{2,1,0:T(8,128)(2,1)S(1)}, u32[]{:S(2)}, u32[]{:S(2)}) %all-to-all-start.2) | async-done | bytes 655392 | tf_op jit(solution)/shard_map/all_to_all | solution.py:258
  182.9 28.6 %all-gather.10.cloned.1.call-done = bf16[3,1024,1024]{2,1,0:T(8,128)(2,1)} async-done(((bf16[3,1024,256]{2,1,0:T(8,128)(2,1)}), bf16[3,1024,1024]{2,1,0:T(8,128)(2,1)}) %all-gather.10.cloned.1.call-update) | async-done | bytes 6291472 | tf_op jit(solution)/shard_map/all_gather | solution.py:249
  211.5 5.0 fusion.50
  241.7 50.8 %all-gather.16.cloned.1.call-done = bf16[1024,4096]{1,0:T(8,128)(2,1)} async-done(((bf16[1024,1024]{1,0:T(8,128)(2,1)}), bf16[1024,4096]{1,0:T(8,128)(2,1)}) %all-gather.16.cloned.1.call-update) | async-done | bytes 8388624 | tf_op jit(solution)/shard_map/all_gather | solution.py:251
  292.5 5.4 fusion.70
  298.0 15.6 %fusion.7 = (bf16[320,4096]{1,0:T(8,128)(2,1)}, f32[320,4096]{1,0:T(8,128)}) fusion(f32[4096]{0:T(1024)S(1)} %convert_element_type.177, f32[320,4096]{1,0:T(8,128)S(1)} %fusion.70, f32[320,128]{1,0:T(8,128)S(1)} %convolution_multiply_fusion.2, bf16[128,4096]{1,0:T(8,128)(2,1)S(1)} %bitcast.152), kind=kOutput, calls=%fused_computation.17 | convolution fusion | flops 2101084160 | bytes 14336000 | tf_op jit(solution)/shard_map/tr,rf->tf/dot_general | solution.py:42
  313.6 38.8 %all-gather.20.cloned.1.call-done = bf16[4096,1024]{1,0:T(8,128)(2,1)} async-done(((bf16[1024,1024]{1,0:T(8,128)(2,1)}), bf16[4096,1024]{1,0:T(8,128)(2,1)}) %all-gather.20.cloned.1.call-update) | async-done | bytes 8388624 | tf_op jit(solution)/shard_map/all_gather | solution.py:252
  352.4 5.9 fusion.47
  358.3 4.8 fusion.4
  385.7 5.6 fusion.33
  391.3 6.2 %multiply_reduce_fusion = (f32[16,320]{1,0:T(8,128)S(1)}, f32[16,320,320]{1,2,0:T(8,128)}) fusion(f32[16,320,320]{1,2,0:T(8,128)} %copy-done.1, f32[16,320]{1,0:T(8,128)S(1)} %log_add_fusion, bf16[320,16,64]{0,2,1:T(8,128)(2,1)S(1)} %bitcast.166, f32[320,16,64]{0,2,1:T(8,128)S(1)} %bitcast.173, f32[16,64]{1,0:T(8,128)S(1)} %add.191), kind=kOutput, calls=%fused_computation.1 | convolution fusion | flops 215280640 | bytes 15118336 | tf_op jit(solution)/shard_map/gqhd,gkhd->ghqk/dot_general | solution.py:38
  397.6 7.1 %multiply_convert_fusion = bf16[16,320,320]{1,2,0:T(8,128)(2,1)S(1)} fusion(f32[16,320,320]{1,2,0:T(8,128)} %get-tuple-element.42, f32[16,320,320]{1,2,0:T(8,128)} %copy-done.1, f32[16,320]{1,0:T(8,128)S(1)} %get-tuple-element.41, f32[16,320]{1,0:T(8,128)S(1)} %log_add_fusion), kind=kLoop, calls=%fused_computation | loop fusion | flops 6553600 | bytes 16424960 | tf_op jit(solution)/shard_map/convert_element_type | solution.py:67
  404.7 3.7 multiply_convert_fusion.1
  425.4 6.3 %fusion.71 = f32[320,1024]{1,0:T(8,128)S(1)} fusion(bf16[320,4096]{1,0:T(8,128)(2,1)} %get-tuple-element.38, bf16[4096,1024]{1,0:T(8,128)(2,1)} %all-gather.20.cloned.1.call-done), kind=kOutput, calls=%fused_computation.145 | convolution fusion | flops 2684354560 | bytes 12320768 | tf_op jit(solution)/shard_map/tf,fd->td/dot_general | solution.py:38
  437.1 5.5 convolution_bitcast_fusion
  445.3 8.1 %all-to-all-done.1 = bf16[320,4,256]{2,0,1:T(8,128)(2,1)S(1)} async-done(((bf16[320,4,256]{2,0,1:T(8,128)(2,1)}), bf16[320,4,256]{2,0,1:T(8,128)(2,1)S(1)}, u32[]{:S(2)}, u32[]{:S(2)}) %all-to-all-start.1) | async-done | bytes 655392 | tf_op jit(solution)/shard_map/all_to_all | solution.py:281
  456.9 10.2 %all-to-all-done.3 = bf16[320,4,256]{2,0,1:T(8,128)(2,1)S(1)} async-done(((bf16[320,4,256]{2,0,1:T(8,128)(2,1)}), bf16[320,4,256]{2,0,1:T(8,128)(2,1)S(1)}, u32[]{:S(2)}, u32[]{:S(2)}) %all-to-all-start.3) | async-done | bytes 655392 | tf_op jit(solution)/shard_map/all_to_all | solution.py:282
  467.1 138.0 %all-reduce.4.cloned.1.call-done = (f32[8,16,1024]{2,1,0:T(8,128)}, f32[8,16,3,1024]{3,1,2,0:T(8,128)}, f32[8,16,1024]{2,1,0:T(8,128)}, f32[8,16,1024]{2,1,0:T(8...) async-done(((f32[8,16,1024]{2,1,0:T(8,128)}, f32[8,16,3,1024]{3,1,2,0:T(8,128)}, ...) | async-done | bytes 8388624 | tf_op jit(solution)/shard_map/psum | solution.py:284
  (250 shorter events, 102.4 us)
Async XLA Ops:
  7.2 290.8 %copy-start = (bf16[8,16,4096]{2,1,0:T(8,128)(2,1)S(1)}, bf16[8,16,4096]{2,1,0:T(8,128)(2,1)}, u32[]{:S(2)}) copy-start(bf16[8,16,4096]{2,1,0:T(8,128)(2,1)} %param.39) | copy-start | bytes 3145732
  7.2 49.9 %all-gather.8.cloned.1.call-start = ((), (), s32[]{:S(2)}) async-start(), calls=%async_computation.4 | async-start | bytes 1769472 | tf_op jit(solution)/shard_map/all_gather | solution.py:243
  7.9 102.1 %all-gather.14.cloned.1.call-start = ((), (), s32[]{:S(2)}) async-start(), calls=%async_computation.7 | async-start | bytes 2359296 | tf_op jit(solution)/shard_map/all_gather | solution.py:245
  8.7 152.3 %all-gather.18.cloned.1.call-start = ((), (), s32[]{:S(2)}) async-start(), calls=%async_computation.9 | async-start | bytes 2359296 | tf_op jit(solution)/shard_map/all_gather | solution.py:246
  9.4 202.1 %all-gather.10.cloned.1.call-start = ((), (), s32[]{:S(2)}) async-start(), calls=%async_computation.5 | async-start | bytes 7864320 | tf_op jit(solution)/shard_map/all_gather | solution.py:249
  57.2 56.4 %copy-start.61 = (bf16[2,256]{1,0:T(2,128)(2,1)S(1)}, bf16[2,256]{1,0:T(2,128)(2,1)}, u32[]{:S(2)}) copy-start(bf16[2,256]{1,0:T(2,128)(2,1)} %param.28) | copy-start | bytes 3076
  57.2 67.5 %copy-start.62 = (s32[4]{0:T(128)S(1)}, s32[4]{0:T(128)}, u32[]{:S(2)}) copy-start(s32[4]{0:T(128)} %param.24) | copy-start | bytes 52
  57.2 67.6 %copy-start.55 = (s32[4,256]{1,0:T(4,128)S(1)}, s32[4,256]{1,0:T(4,128)}, u32[]{:S(2)}) copy-start(s32[4,256]{1,0:T(4,128)} %param.23) | copy-start | bytes 12292
  57.2 67.8 %copy-start.60 = (bf16[1024]{0:T(1024)(128)(2,1)S(1)}, bf16[1024]{0:T(1024)(128)(2,1)}, u32[]{:S(2)}) copy-start(bf16[1024]{0:T(1024)(128)(2,1)} %param.31) | copy-start | bytes 6148
  57.2 72.9 %copy-start.59 = (f32[2,1024]{1,0:T(2,128)S(1)}, f32[2,1024]{1,0:T(2,128)}, u32[]{:S(2)}) copy-start(f32[2,1024]{1,0:T(2,128)} %param.25) | copy-start | bytes 24580
  57.2 73.1 %copy-start.58 = (f32[2,1024]{1,0:T(2,128)S(1)}, f32[2,1024]{1,0:T(2,128)}, u32[]{:S(2)}) copy-start(f32[2,1024]{1,0:T(2,128)} %param.26) | copy-start | bytes 24580
  57.2 73.1 %copy-start.35 = (bf16[8,16,3,1024]{3,1,2,0:T(8,128)(2,1)S(1)}, bf16[8,16,3,1024]{3,1,2,0:T(8,128)(2,1)}, u32[]{:S(2)}) copy-start(bf16[8,16,3,1024]{3,1,2,0:T(8,128)(2,1)} %param.35) | copy-start | bytes 2359300
  57.2 177.9 %all-gather.12.cloned.1.call-start = ((), (), s32[]{:S(2)}) async-start(), calls=%async_computation.6 | async-start | bytes 2621440 | tf_op jit(solution)/shard_map/all_gather | solution.py:250
  88.1 204.4 %all-gather.16.cloned.1.call-start = ((), (), s32[]{:S(2)}) async-start(), calls=%async_computation.8 | async-start | bytes 10485760 | tf_op jit(solution)/shard_map/all_gather | solution.py:251
  110.0 51.0 %copy-start.56 = (bf16[2,1024]{1,0:T(2,128)(2,1)S(1)}, bf16[2,1024]{1,0:T(2,128)(2,1)}, u32[]{:S(2)}) copy-start(bf16[2,1024]{1,0:T(2,128)(2,1)} %param.33) | copy-start | bytes 12292
  110.0 51.6 %all-to-all-start = ((bf16[4,320,256]{2,1,0:T(8,128)(2,1)}), bf16[4,320,256]{2,1,0:T(8,128)(2,1)S(1)}, u32[]{:S(2)}, u32[]{:S(2)}) async-start(bf16[4,320,256]{2,1,0:T(8,128)(2,1)} %bitcast), calls=%async_computation | async-start | bytes 1310720 | tf_op jit(solution)/shard_map/all_to_all | solution.py:257
  113.5 238.8 %all-gather.20.cloned.1.call-start = ((), (), s32[]{:S(2)}) async-start(), calls=%async_computation.10 | async-start | bytes 10485760 | tf_op jit(solution)/shard_map/all_gather | solution.py:252
  130.2 52.5 %copy-start.53 = (f32[1,1024]{1,0:T(1,128)}, f32[1,1024]{1,0:T(1,128)S(1)}, u32[]{:S(2)}) copy-start(f32[1,1024]{1,0:T(1,128)S(1)} %get-tuple-element.44) | copy-start | bytes 12292
  161.6 17.9 %all-to-all-start.2 = ((bf16[4,320,256]{2,1,0:T(8,128)(2,1)}), bf16[4,320,256]{2,1,0:T(8,128)(2,1)S(1)}, u32[]{:S(2)}, u32[]{:S(2)}) async-start(bf16[4,320,256]{2,1,0:T(8,128)(2,1)} %bitcast.201), calls=%async_computation.2 | async-start | bytes 1310720 | tf_op jit(solution)/shard_map/all_to_all | solution.py:258
  165.1 440.0 %all-reduce.4.cloned.1.call-start = ((), (), s32[]{:S(2)}) async-start(), calls=%async_computation.11 | async-start | bytes 16777216 | tf_op jit(solution)/shard_map/psum | solution.py:284
  181.6 34.9 %copy-start.42 = (f32[320,128,1]{1,0,2:T(8,128)}, f32[320,128,1]{1,0,2:T(8,128)S(1)}, u32[]{:S(2)}) copy-start(f32[320,128,1]{1,0,2:T(8,128)S(1)} %fusion.46) | copy-start | bytes 491524
  182.9 33.6 %copy-start.17 = (bf16[8,16,3,1024]{3,1,0,2:T(8,128)(2,1)S(1)}, bf16[8,16,3,1024]{3,1,0,2:T(8,128)(2,1)}, u32[]{:S(2)}) copy-start(bf16[8,16,3,1024]{3,1,0,2:T(8,128)(2,1)} %copy.85) | copy-start | bytes 2359300
  433.5 19.9 %all-to-all-start.1 = ((bf16[320,4,256]{2,0,1:T(8,128)(2,1)}), bf16[320,4,256]{2,0,1:T(8,128)(2,1)S(1)}, u32[]{:S(2)}, u32[]{:S(2)}) async-start(bf16[320,4,256]{2,0,1:T(8,128)(2,1)} %bitcast.151), calls=%async_computation.1 | async-start | bytes 1310720 | tf_op jit(solution)/shard_map/all_to_all | solution.py:281
  453.4 13.7 %all-to-all-start.3 = ((bf16[320,4,256]{2,0,1:T(8,128)(2,1)}), bf16[320,4,256]{2,0,1:T(8,128)(2,1)S(1)}, u32[]{:S(2)}, u32[]{:S(2)}) async-start(bf16[320,4,256]{2,0,1:T(8,128)(2,1)} %bitcast.150), calls=%async_computation.3 | async-start | bytes 1310720 | tf_op jit(solution)/shard_map/all_to_all | solution.py:282
  (55 other events, 263.9 us)
Sparse Core Ops, SparseCore 0:
  10.2 46.9 all-gather.7
  59.3 50.6 all-gather.13
  112.1 48.8 all-gather.17
  162.4 49.1 all-gather.9
  212.9 19.8 all-gather.11
  234.2 58.2 all-gather.15
  294.1 58.2 all-gather.19
  425.5 179.4 all-reduce.3
where the time goes:
time: 631 us; the launch traced here: 622 us
  waiting for transfers between devices  388 us (61%)
  matrix products  107 us (17%)
  blocking collectives  47 us (7%)
  local copies, waits for them, and re-layouts  38.4 us (6%)
  between operations  15.4 us (2%)
  starting transfers between devices  14.3 us (2%)
  other arithmetic  11.5 us (2%)
    psum x1, waiting for transfers between devices, per_device(): lax.psum((grads[0], grads[1], grads[2], grads[3], grads[4], grads[5], gra...  138 us
    dot_general x22, matrix products, narrow_dot(): jnp.einsum(formula, left_side, right_side, preferred_element_type=jnp.flo...  62.1 us
    all_gather x1, waiting for transfers between devices, per_device(): lax.all_gather(fc1_cols, 'col', axis=1, tiled=True)  50.8 us
    all_gather x1, waiting for transfers between devices, per_device(): lax.all_gather(w_qkv, 'row', axis=1, tiled=True)  47.7 us
    dot_general x16, matrix products, exact_dot(): jnp.einsum(formula, left_side, right_side, precision=highest, preferred_e...  45.2 us
    all_gather x1, waiting for transfers between devices, per_device(): lax.all_gather(fc2_rows, 'col', axis=0, tiled=True)  38.8 us
    all_gather x1, blocking collectives, per_device(): lax.all_gather(w_proj, 'row', axis=1, tiled=True)  30.8 us
    all_gather x1, waiting for transfers between devices, per_device(): lax.all_gather(w_fc2, 'row', axis=1, tiled=True)  29.4 us
  transfers between devices with their start and end apart: 12, of which 10 were waited for; matrix products, arithmetic and copies ran while one was open for 11% of the time, Pallas kernels for 0%

commit v1 on v0

--- a/solution.py
+++ b/solution.py
@@ -12,6 +12,22 @@
 NA = 8
 SEQ = 320
 highest = lax.Precision.HIGHEST
+
+
+def collect(x, axis, dim):
+    ways, here, step = (lax.axis_size(axis), lax.axis_index(axis), x.shape[dim])
+    dims = [n * ways if d == dim else n for d, n in enumerate(x.shape)]
+    full = lax.dynamic_update_slice_in_dim(jnp.zeros(dims, x.dtype), x, here * step, axis=dim)
+    going_up = going_down = x
+    for far in range(1, ways // 2 + 1):
+        going_up = lax.ppermute(going_up, axis, [(d, (d + 1) % ways) for d in range(ways)])
+        full = lax.dynamic_update_slice_in_dim(full, going_up, (here - far) % ways * step, axis=dim)
+        if 2 * far < ways:
+            going_down = lax.ppermute(going_down, axis, [(d, (d - 1) % ways) for d in range(ways)])
+            full = lax.dynamic_update_slice_in_dim(
+                full, going_down, (here + far) % ways * step, axis=dim
+            )
+    return full
 
 
 def norm_parts(values):
@@ -243,7 +259,7 @@
         lax.all_gather(w_qkv, "row", axis=1, tiled=True),
         lax.all_gather(w_proj, "row", axis=1, tiled=True),
         lax.all_gather(w_fc1, "row", axis=0, tiled=True),
-        lax.all_gather(w_fc2, "row", axis=1, tiled=True),
+        collect(w_fc2, "row", 1),
     )
     qkv_full, proj_full, fc1_full, fc2_full, bias_qv_full, bias_fc1_full = (
         lax.all_gather(qkv_cols, "col", axis=2, tiled=True),

time: 631 us -> 583 us (0.924)
  waiting for transfers between devices: 388 us -> 287 us
  local copies, waits for them, and re-layouts: 38.4 us -> 65.3 us
  starting transfers between devices: 14.3 us -> 29.6 us
    all_gather x1, waiting for transfers between devices: 50.8 us -> 14 us  [per_device(): lax.all_gather(fc1_cols, 'col', axis=1, tiled=True)]
    all_gather x1 -> x0, waiting for transfers between devices: 29.4 us -> none  [per_device(): lax.all_gather(w_fc2, 'row', axis=1, tiled=True)]
    all_gather x1, waiting for transfers between devices: 28.6 us -> 0.01 us  [per_device(): lax.all_gather(qkv_cols, 'col', axis=2, tiled=True)]
    ppermute x0 -> x7, starting transfers between devices: none -> 14.6 us  [the longest x3 13 us: collect(): lax.ppermute(going_down, axis, [(d, (d - 1) % ways) for d in range(ways)])]
    all_to_all x1, waiting for transfers between devices: 12.3 us -> 0.01 us  [per_device(): lax.all_to_all(grad_out, 'col', split_axis=0, concat_axis=1, tiled=True)]
    ppermute x0 -> x7, waiting for transfers between devices: none -> 8.84 us  [the longest x4 4.91 us: collect(): lax.ppermute(going_up, axis, [(d, (d + 1) % ways) for d in range(ways)])]
    dot_general x22, matrix products: 62.1 us -> 70 us  [narrow_dot(): jnp.einsum(formula, left_side, right_side, preferred_element_type=jnp.flo...]
    unnamed x145 -> x177, local copies, waits for them, and re-layouts: 16.4 us -> 20.4 us
  transfers between devices with their start and end apart: 12 -> 18, of which waited for: 10 -> 10; matrix products, arithmetic and copies ran while one was open for 11% -> 18% of each run, Pallas kernels for 0% -> 0%
where the time goes in v1:
time: 583 us; the launch traced here: 579 us
  waiting for transfers between devices  287 us (49%)
  matrix products  113 us (19%)
  local copies, waits for them, and re-layouts  65.3 us (11%)
  blocking collectives  52.9 us (9%)
  starting transfers between devices  29.6 us (5%)
  other arithmetic  15.4 us (3%)
  between operations  15.3 us (3%)
    psum x1, waiting for transfers between devices, per_device(): lax.psum((grads[0], grads[1], grads[2], grads[3], grads[4], grads[5], gra...  138 us
    dot_general x22, matrix products, narrow_dot(): jnp.einsum(formula, left_side, right_side, preferred_element_type=jnp.flo...  70 us
    all_gather x1, waiting for transfers between devices, per_device(): lax.all_gather(w_qkv, 'row', axis=1, tiled=True)  48.4 us
    dot_general x16, matrix products, exact_dot(): jnp.einsum(formula, left_side, right_side, precision=highest, preferred_e...  43.4 us
    all_gather x1, waiting for transfers between devices, per_device(): lax.all_gather(fc2_rows, 'col', axis=0, tiled=True)  39.1 us
    all_gather x1, blocking collectives, per_device(): lax.all_gather(w_proj, 'row', axis=1, tiled=True)  31 us
    all_gather x1, waiting for transfers between devices, per_device(): lax.all_gather(w_fc1, 'row', axis=0, tiled=True)  21.5 us
    unnamed x177, local copies, waits for them, and re-layouts  20.4 us
  transfers between devices with their start and end apart: 18, of which 10 were waited for; matrix products, arithmetic and copies ran while one was open for 18% of the time, Pallas kernels for 0%

profile of v1, /device:TPU:0, one launch (start us, length us, event | category | flops | bytes accessed | tf_op | source)
XLA Modules:
  0.0 579.3 jit_solution(6423102766796706566)
XLA Ops:
  8.7 48.4 %all-gather.7.cloned.1.call-done = bf16[3,1024,256]{2,1,0:T(8,128)(2,1)} async-done(((bf16[3,128,256]{2,1,0:T(8,128)(2,1)}), bf16[3,1024,256]{2,1,0:T(8,128)(2,1)}) %all-gather.7.cloned.1.call-update) | async-done | bytes 1572880 | tf_op jit(solution)/shard_map/all_gather | solution.py:259
  57.2 31.0 %all_gather.30 = bf16[256,1024]{1,0:T(8,128)(2,1)} all-gather(bf16[256,128]{1,0:T(8,128)(2,1)} %param.29), channel_id=1, replica_groups=mesh['row'=8,'col'=4] {'row'}, dimensions={1}, use_global_device_ids=true | all-gather | bytes 589824 | tf_op jit(solution)/shard_map/all_gather | solution.py:260
  88.3 21.5 %all-gather.13.cloned.1.call-done = bf16[1024,1024]{1,0:T(8,128)(2,1)} async-done(((bf16[128,1024]{1,0:T(8,128)(2,1)}), bf16[1024,1024]{1,0:T(8,128)(2,1)}) %all-gather.13.cloned.1.call-update) | async-done | bytes 2097168 | tf_op jit(solution)/shard_map/all_gather | solution.py:261
  115.6 16.5 %all_gather.29 = bf16[2,1024]{1,0:T(2,128)(2,1)S(1)} all-gather(bf16[2,256]{1,0:T(2,128)(2,1)S(1)} %copy-done.81), channel_id=1, replica_groups=mesh['row'=8,'col'=4] {'col'}, dimensions={1}, use_global_device_ids=true | all-gather | bytes 5120 | tf_op jit(solution)/shard_map/all_gather | solution.py:269
  142.7 5.5 all_gather.34
  166.7 7.6 %collective-permute-start.5 = (bf16[1024,128]{1,0:T(8,128)(2,1)S(1)}, bf16[1024,128]{1,0:T(8,128)(2,1)S(1)}, u32[]{:S(2)}, u32[]{:S(2)}) collective-permute-start(bf16[1024,128]{1,0:T(8,128)(2,1)S(1)} %collective-permute-done.3), channel_id=1, source_target_pairs={{0,28},{4,0},{8,4},{12,8},{16,12},{20,16},{24,20},{28,24},{1,29},{... | collective-permute-start | bytes 786440 | tf_op jit(solution)/shard_map/ppermute | solution.py:26
  180.3 4.9 collective-permute-done.6
  192.4 4.6 fusion.72
  197.0 6.2 %fusion.49 = f32[320,3,1024]{2,0,1:T(8,128)S(1)} fusion(bf16[3,1024,1024]{2,1,0:T(8,128)(2,1)} %all-gather.9.cloned.1.call-done, bf16[320,1024]{1,0:T(8,128)(2,1)} %add_convert_fusion.4), kind=kOutput, calls=%fused_computation.102 | convolution fusion | flops 2013265920 | bytes 10878976 | tf_op jit(solution)/shard_map/td,cde->cte/dot_general | solution.py:54
  209.3 3.8 fusion.63
  234.7 14.0 %all-gather.15.cloned.1.call-done = bf16[1024,4096]{1,0:T(8,128)(2,1)} async-done(((bf16[1024,1024]{1,0:T(8,128)(2,1)}), bf16[1024,4096]{1,0:T(8,128)(2,1)}) %all-gather.15.cloned.1.call-update) | async-done | bytes 8388624 | tf_op jit(solution)/shard_map/all_gather | solution.py:267
  248.7 5.5 fusion.70
  254.2 15.6 %fusion.7 = (bf16[320,4096]{1,0:T(8,128)(2,1)}, f32[320,4096]{1,0:T(8,128)}) fusion(f32[4096]{0:T(1024)S(1)} %copy-done.71, f32[320,4096]{1,0:T(8,128)S(1)} %fusion.70, f32[320,128]{1,0:T(8,128)S(1)} %copy-done.37, bf16[128,4096]{1,0:T(8,128)(2,1)S(1)} %bitcast.152), kind=kOutput, calls=%fused_computation.17 | convolution fusion | flops 2101084160 | bytes 14336000 | tf_op jit(solution)/shard_map/tr,rf->tf/dot_general | solution.py:58
  269.9 39.1 %all-gather.17.cloned.1.call-done = bf16[4096,1024]{1,0:T(8,128)(2,1)} async-done(((bf16[1024,1024]{1,0:T(8,128)(2,1)}), bf16[4096,1024]{1,0:T(8,128)(2,1)}) %all-gather.17.cloned.1.call-update) | async-done | bytes 8388624 | tf_op jit(solution)/shard_map/all_gather | solution.py:268
  309.0 9.6 %fusion.4 = bf16[320,4096]{1,0:T(8,128)(2,1)S(1)} fusion(f32[320,4096]{1,0:T(8,128)} %fusion.72, bf16[4096,1024]{1,0:T(8,128)(2,1)} %all-gather.17.cloned.1.call-done, f32[320,4096]{1,0:T(8,128)} %get-tuple-element.39, f32[320,1024]{1,0:T(8,128)} %bitcast.160, f32[320]{0:T(512)S(1)} %copy-done.63), kind=kOutput, calls=%fused_computation.14 | convolution fusion | flops 2699427840 | bytes 22807808 | tf_op jit(solution)/shard_map/td,fd->tf/dot_general | solution.py:54
  342.3 5.6 fusion.30
  347.8 6.3 %multiply_reduce_fusion = (f32[16,320]{1,0:T(8,128)S(1)}, f32[16,320,320]{1,2,0:T(8,128)}) fusion(f32[16,320,320]{1,2,0:T(8,128)} %copy-done.1, f32[16,320]{1,0:T(8,128)S(1)} %log_add_fusion, bf16[320,16,64]{0,2,1:T(8,128)(2,1)S(1)} %bitcast.166, f32[320,16,64]{0,2,1:T(8,128)S(1)} %bitcast.173, f32[16,64]{1,0:T(8,128)S(1)} %copy-done.65), kind=kOutput, calls=%fused_computation.1 | convolution fusion | flops 215280640 | bytes 15118336 | tf_op jit(solution)/shard_map/gqhd,gkhd->ghqk/dot_general | solution.py:54
  354.1 7.1 %multiply_convert_fusion = bf16[16,320,320]{1,2,0:T(8,128)(2,1)S(1)} fusion(f32[16,320,320]{1,2,0:T(8,128)} %get-tuple-element.42, f32[16,320,320]{1,2,0:T(8,128)} %copy-done.1, f32[16,320]{1,0:T(8,128)S(1)} %get-tuple-element.41, f32[16,320]{1,0:T(8,128)S(1)} %log_add_fusion), kind=kLoop, calls=%fused_computation | loop fusion | flops 6553600 | bytes 16424960 | tf_op jit(solution)/shard_map/convert_element_type | solution.py:83
  361.3 3.7 multiply_convert_fusion.1
  383.6 7.6 %fusion.36 = bf16[320,1024]{1,0:T(8,128)(2,1)S(1)} fusion(f32[320,1024]{1,0:T(8,128)} %copy-done.2, f32[320,1024]{1,0:T(8,128)S(1)} %fusion.71, bf16[320,4096]{1,0:T(8,128)(2,1)} %get-tuple-element.38, bf16[4096,1024]{1,0:T(8,128)(2,1)} %all-gather.17.cloned.1.call-done, f32[1024]{0:T(1024)S(1)} %bitcast.212, f32[320]{0:T(512)S(1)} %copy-done.63), kind=kOutput, calls=%fused_computation.68 | convolution fusion | flops 2685992960 | bytes 14292224 | tf_op jit(solution)/shard_map/tf,fd->td/dot_general | solution.py:54
  395.8 5.8 %convolution_bitcast_fusion = f32[320,1024]{1,0:T(8,128)S(1)} fusion(bf16[3,1024,1024]{2,1,0:T(8,128)(2,1)} %all-gather.9.cloned.1.call-done, bf16[1,320,1024]{2,1,0:T(8,128)(2,1)} %copy.99, bf16[1,320,1024]{2,1,0:T(8,128)(2,1)} %copy.98, bf16[1,320,1024]{2,1,0:T(8,128)(2,1)} %copy.97), kind=kOutput, calls=%fused_computation.61 | convolution fusion | flops 2015232000 | bytes 9568256 | tf_op jit(solution)/shard_map/cte,cde->td/dot_general | solution.py:54
  404.3 5.7 all-to-all-done.1
  413.4 10.2 %all-to-all-done.3 = bf16[320,4,256]{2,0,1:T(8,128)(2,1)S(1)} async-done(((bf16[320,4,256]{2,0,1:T(8,128)(2,1)}), bf16[320,4,256]{2,0,1:T(8,128)(2,1)S(1)}, u32[]{:S(2)}, u32[]{:S(2)}) %all-to-all-start.3) | async-done | bytes 655392 | tf_op jit(solution)/shard_map/all_to_all | solution.py:298
  423.6 138.1 %all-reduce.4.cloned.1.call-done = (f32[8,16,1024]{2,1,0:T(8,128)}, f32[8,16,3,1024]{3,1,2,0:T(8,128)}, f32[8,16,1024]{2,1,0:T(8,128)}, f32[8,16,1024]{2,1,0:T(8...) async-done(((f32[8,16,1024]{2,1,0:T(8,128)}, f32[8,16,3,1024]{3,1,2,0:T(8,128)}, ...) | async-done | bytes 8388624 | tf_op jit(solution)/shard_map/psum | solution.py:300
  (301 shorter events, 140.1 us)
Async XLA Ops:
  7.2 247.0 %copy-start = (bf16[8,16,4096]{2,1,0:T(8,128)(2,1)S(1)}, bf16[8,16,4096]{2,1,0:T(8,128)(2,1)}, u32[]{:S(2)}) copy-start(bf16[8,16,4096]{2,1,0:T(8,128)(2,1)} %param.39) | copy-start | bytes 3145732
  7.2 49.9 %all-gather.7.cloned.1.call-start = ((), (), s32[]{:S(2)}) async-start(), calls=%async_computation.4 | async-start | bytes 1769472 | tf_op jit(solution)/shard_map/all_gather | solution.py:259
  7.9 101.9 %all-gather.13.cloned.1.call-start = ((), (), s32[]{:S(2)}) async-start(), calls=%async_computation.7 | async-start | bytes 2359296 | tf_op jit(solution)/shard_map/all_gather | solution.py:261
  8.7 188.3 %all-gather.9.cloned.1.call-start = ((), (), s32[]{:S(2)}) async-start(), calls=%async_computation.5 | async-start | bytes 7864320 | tf_op jit(solution)/shard_map/all_gather | solution.py:265
  57.1 52.7 %copy-start.49 = (bf16[1024,128]{1,0:T(8,128)(2,1)S(1)}, bf16[1024,128]{1,0:T(8,128)(2,1)}, u32[]{:S(2)}) copy-start(bf16[1024,128]{1,0:T(8,128)(2,1)} %param.32) | copy-start | bytes 786436
  57.2 170.9 %all-gather.11.cloned.1.call-start = ((), (), s32[]{:S(2)}) async-start(), calls=%async_computation.6 | async-start | bytes 2621440 | tf_op jit(solution)/shard_map/all_gather | solution.py:266
  88.2 46.8 %copy-start.72 = (s32[4,256]{1,0:T(4,128)S(1)}, s32[4,256]{1,0:T(4,128)}, u32[]{:S(2)}) copy-start(s32[4,256]{1,0:T(4,128)} %param.23) | copy-start | bytes 12292
  88.3 160.5 %all-gather.15.cloned.1.call-start = ((), (), s32[]{:S(2)}) async-start(), calls=%async_computation.8 | async-start | bytes 10485760 | tf_op jit(solution)/shard_map/all_gather | solution.py:267
  109.9 47.4 %collective-permute-start.1 = (bf16[1024,128]{1,0:T(8,128)(2,1)S(1)}, bf16[1024,128]{1,0:T(8,128)(2,1)S(1)}, u32[]{:S(2)}, u32[]{:S(2)}) collective-permute-start(bf16[1024,128]{1,0:T(8,128)(2,1)S(1)} %copy-done.49), channel_id=1, source_target_pairs={{0,28},{4,0},{8,4},{12,8},{16,12},{20,16},{24,20},{28,24},{1,29},{... | collective-permute-start | bytes 786440 | tf_op jit(solution)/shard_map/ppermute | solution.py:26
  111.8 26.3 %collective-permute-start = (bf16[1024,128]{1,0:T(8,128)(2,1)S(1)}, bf16[1024,128]{1,0:T(8,128)(2,1)S(1)}, u32[]{:S(2)}, u32[]{:S(2)}) collective-permute-start(bf16[1024,128]{1,0:T(8,128)(2,1)S(1)} %copy-done.49), channel_id=1, source_target_pairs={{0,4},{4,8},{8,12},{12,16},{16,20},{20,24},{24,28},{28,0},{1,5},{5... | collective-permute-start | bytes 786440 | tf_op jit(solution)/shard_map/ppermute | solution.py:23
  111.9 50.1 %all-to-all-start = ((bf16[4,320,256]{2,1,0:T(8,128)(2,1)}), bf16[4,320,256]{2,1,0:T(8,128)(2,1)S(1)}, u32[]{:S(2)}, u32[]{:S(2)}) async-start(bf16[4,320,256]{2,1,0:T(8,128)(2,1)} %bitcast), calls=%async_computation | async-start | bytes 1310720 | tf_op jit(solution)/shard_map/all_to_all | solution.py:273
  134.4 56.8 %copy-start.56 = (f32[1,1024]{1,0:T(1,128)}, f32[1,1024]{1,0:T(1,128)S(1)}, u32[]{:S(2)}) copy-start(f32[1,1024]{1,0:T(1,128)S(1)} %get-tuple-element.44) | copy-start | bytes 12292
  138.0 24.1 %collective-permute-start.2 = (bf16[1024,128]{1,0:T(8,128)(2,1)S(1)}, bf16[1024,128]{1,0:T(8,128)(2,1)S(1)}, u32[]{:S(2)}, u32[]{:S(2)}) collective-permute-start(bf16[1024,128]{1,0:T(8,128)(2,1)S(1)} %collective-permute-done), channel_id=1, source_target_pairs={{0,4},{4,8},{8,12},{12,16},{16,20},{20,24},{24,28},{28,0},{1,5},{5... | collective-permute-start | bytes 786440 | tf_op jit(solution)/shard_map/ppermute | solution.py:23
  151.5 67.4 %copy-start.52 = (f32[16,64]{1,0:T(8,128)}, f32[16,64]{1,0:T(8,128)S(1)}, u32[]{:S(2)}) copy-start(f32[16,64]{1,0:T(8,128)S(1)} %add.254) | copy-start | bytes 12292
  157.2 9.5 %collective-permute-start.3 = (bf16[1024,128]{1,0:T(8,128)(2,1)S(1)}, bf16[1024,128]{1,0:T(8,128)(2,1)S(1)}, u32[]{:S(2)}, u32[]{:S(2)}) collective-permute-start(bf16[1024,128]{1,0:T(8,128)(2,1)S(1)} %collective-permute-done.1), channel_id=1, source_target_pairs={{0,28},{4,0},{8,4},{12,8},{16,12},{20,16},{24,20},{28,24},{1,29},{... | collective-permute-start | bytes 786440 | tf_op jit(solution)/shard_map/ppermute | solution.py:26
  162.1 13.0 %collective-permute-start.4 = (bf16[1024,128]{1,0:T(8,128)(2,1)S(1)}, bf16[1024,128]{1,0:T(8,128)(2,1)S(1)}, u32[]{:S(2)}, u32[]{:S(2)}) collective-permute-start(bf16[1024,128]{1,0:T(8,128)(2,1)S(1)} %collective-permute-done.2), channel_id=1, source_target_pairs={{0,4},{4,8},{8,12},{12,16},{16,20},{20,24},{24,28},{28,0},{1,5},{5... | collective-permute-start | bytes 786440 | tf_op jit(solution)/shard_map/ppermute | solution.py:23
  162.1 26.3 %all-to-all-start.2 = ((bf16[4,320,256]{2,1,0:T(8,128)(2,1)}), bf16[4,320,256]{2,1,0:T(8,128)(2,1)S(1)}, u32[]{:S(2)}, u32[]{:S(2)}) async-start(bf16[4,320,256]{2,1,0:T(8,128)(2,1)} %bitcast.203), calls=%async_computation.2 | async-start | bytes 1310720 | tf_op jit(solution)/shard_map/all_to_all | solution.py:274
  165.6 143.4 %all-gather.17.cloned.1.call-start = ((), (), s32[]{:S(2)}) async-start(), calls=%async_computation.9 | async-start | bytes 10485760 | tf_op jit(solution)/shard_map/all_gather | solution.py:268
  166.7 12.9 %collective-permute-start.5 = (bf16[1024,128]{1,0:T(8,128)(2,1)S(1)}, bf16[1024,128]{1,0:T(8,128)(2,1)S(1)}, u32[]{:S(2)}, u32[]{:S(2)}) collective-permute-start(bf16[1024,128]{1,0:T(8,128)(2,1)S(1)} %collective-permute-done.3), channel_id=1, source_target_pairs={{0,28},{4,0},{8,4},{12,8},{16,12},{20,16},{24,20},{28,24},{1,29},{... | collective-permute-start | bytes 786440 | tf_op jit(solution)/shard_map/ppermute | solution.py:26
  175.1 10.1 %collective-permute-start.6 = (bf16[1024,128]{1,0:T(8,128)(2,1)S(1)}, bf16[1024,128]{1,0:T(8,128)(2,1)S(1)}, u32[]{:S(2)}, u32[]{:S(2)}) collective-permute-start(bf16[1024,128]{1,0:T(8,128)(2,1)S(1)} %collective-permute-done.4), channel_id=1, source_target_pairs={{0,4},{4,8},{8,12},{12,16},{16,20},{20,24},{24,28},{28,0},{1,5},{5... | collective-permute-start | bytes 786440 | tf_op jit(solution)/shard_map/ppermute | solution.py:23
  185.9 375.8 %all-reduce.4.cloned.1.call-start = ((), (), s32[]{:S(2)}) async-start(), calls=%async_computation.10 | async-start | bytes 16777216 | tf_op jit(solution)/shard_map/psum | solution.py:300
  254.2 54.8 %copy-start.63 = (f32[320]{0:T(512)S(1)}, f32[320]{0:T(512)}, u32[]{:S(2)}) copy-start(f32[320]{0:T(512)} %fusion.54) | copy-start | bytes 3844
  392.1 17.9 %all-to-all-start.1 = ((bf16[320,4,256]{2,0,1:T(8,128)(2,1)}), bf16[320,4,256]{2,0,1:T(8,128)(2,1)S(1)}, u32[]{:S(2)}, u32[]{:S(2)}) async-start(bf16[320,4,256]{2,0,1:T(8,128)(2,1)} %bitcast.181), calls=%async_computation.1 | async-start | bytes 1310720 | tf_op jit(solution)/shard_map/all_to_all | solution.py:297
  410.0 13.7 %all-to-all-start.3 = ((bf16[320,4,256]{2,0,1:T(8,128)(2,1)}), bf16[320,4,256]{2,0,1:T(8,128)(2,1)S(1)}, u32[]{:S(2)}, u32[]{:S(2)}) async-start(bf16[320,4,256]{2,0,1:T(8,128)(2,1)} %bitcast.150), calls=%async_computation.3 | async-start | bytes 1310720 | tf_op jit(solution)/shard_map/all_to_all | solution.py:298
  (77 other events, 470.0 us)
Sparse Core Ops, SparseCore 0:
  10.2 46.9 all-gather.6
  59.3 50.5 all-gather.12
  111.4 50.6 all-gather.8
  163.5 25.0 all-gather.10
  190.0 58.7 all-gather.14
  250.7 58.2 all-gather.16
  382.1 179.5 all-reduce.3
